TPU v7x, 256 devices: a whole 4x4x8 slice. The times are simulated.
256 devices in a mesh: kv: 8 (over x, core), seq: 8 (over z), vocab: 4 (over y).
Axes of the slice: x: 4, y: 4, z: 8, core: 2. Of those that a mesh axis runs over, the one named last changes fastest.
Arguments:
- hidden_state: bfloat16 [48, 4, 3584], P('kv', 'vocab', 'seq'), may hold values from -6 to 6
- input_projection: bfloat16 [3584, 8, 1024], P('seq', 'kv'), may hold values from -0.09375 to 0.09375
- output_projection: bfloat16 [8, 512, 3584], P('kv', None, 'seq'), may hold values from -0.09375 to 0.09375
- norm_pre_attention: float32 [3584], P('seq'), may hold values from 0.1 to 1.9
- norm_post_attention: float32 [3584], P('seq'), may hold values from 0.1 to 1.9
- norm_pre_feedforward: float32 [3584], P('seq'), may hold values from 0.1 to 1.9
- norm_post_feedforward: float32 [3584], P('seq'), may hold values from 0.1 to 1.9
- norm_final: float32 [3584], P('seq'), may hold values from 0.1 to 1.9
- cache_keys: bfloat16 [4, 16384, 8, 256], P('vocab', 'seq', 'kv')
- cache_values: bfloat16 [4, 16384, 8, 256], P('vocab', 'seq', 'kv')
- cache_length: int32 [4], P('vocab'), may hold values from 1 to 16379, as said below
- ancestors: int32 [4, 48, 48], P('vocab'), may hold values from 0 to 1, as said below
- accepted_path: int32 [4, 5], P('vocab'), may hold values from 0 to 47, as said below
- gate_up_weight: bfloat16 [3584, 2, 14336], P('seq', None, ('kv', 'vocab')), may hold values from -0.09375 to 0.09375
- down_weight: bfloat16 [14336, 3584], P(('kv', 'vocab'), 'seq'), may hold values from -0.046875 to 0.046875
- draft_weight: bfloat16 [4, 3584, 3584], P(None, 'seq', ('kv', 'vocab')), may hold values from -0.09375 to 0.09375
- draft_bias: float32 [4, 3584], P(None, ('kv', 'vocab')), may hold values from -3 to 3
- vocab_weight: bfloat16 [131072, 3584], P(('kv', 'seq', 'vocab'))
- candidate_tokens: int32 [5, 48, 4, 8], replicated, may hold values from 0 to 131071
Outputs:
- keys_updated: bfloat16 [4, 16384, 8, 256], P('vocab', 'seq', 'kv')
- values_updated: bfloat16 [4, 16384, 8, 256], P('vocab', 'seq', 'kv')
- log_normalizer: float32 [5, 48, 4], replicated
- candidate_logits: float32 [5, 48, 4, 8], replicated
Inputs may be any that keep to these rules, and one draw needn't show every extreme that they name: The first cache_length[k] slots of tenant k's cache are filled; in every draw some tenant holds exactly 16379. ancestors[k, t, u] is 1 exactly when u is t or an ancestor of t in tenant k's tree; node 0 is the root and every parent has a lower index than its child. accepted_path[k] lists 5 nodes of tenant k's tree from the root down, each the parent of the next; the last of them is node 47.
All inputs are finite; a program needn't handle non-finite values.
Results may differ from a plain program's by a relative error of at most 0.02.
Values may be sent and summed in bfloat16 or wider, within the bound.
A program may use at most 64 MiB of HBM per device.

v0:
```python
import jax
import jax.numpy as jnp
from jax import lax
from jax.sharding import PartitionSpec as P

MODEL_WIDTH = 3584
HEAD_SIZE = 256
CAND = 8
EPSILON = 1e-06
SCORE_CAP = 50.0
LOGIT_CAP = 30.0


def apply_rotary(vectors, token_positions):
    half_dim = vectors.shape[-1] // 2
    frequency = 10000.0 ** (-2.0 * jnp.arange(half_dim, dtype=jnp.float32) / vectors.shape[-1])
    angles = token_positions.astype(jnp.float32)[..., None] * frequency
    cosine = jnp.cos(angles)
    sine_part = jnp.sin(angles)
    first_half = vectors[..., :half_dim]
    second_half = vectors[..., half_dim:]
    return jnp.concatenate(
        [
            first_half * cosine - second_half * sine_part,
            second_half * cosine + first_half * sine_part,
        ],
        axis=-1,
    )


def capped_weight(scores):
    return jnp.exp(SCORE_CAP * jnp.tanh(scores * 0.0625 / SCORE_CAP))


def row_inverse(values):
    totals = lax.psum(jnp.sum(values * values, axis=-1), "seq")
    return lax.rsqrt(totals / MODEL_WIDTH + EPSILON)[:, None]


def gated_units(gate_up, squares):
    inverse = lax.rsqrt(squares / MODEL_WIDTH + EPSILON)[:, None]
    return (
        jax.nn.gelu(gate_up[:, 0] * inverse, approximate=True) * (gate_up[:, 1] * inverse)
    ).astype(jnp.bfloat16)


def local(
    hidden_state,
    input_projection,
    output_projection,
    norm_pre_attention,
    norm_post_attention,
    norm_pre_feedforward,
    norm_post_feedforward,
    norm_final,
    cache_keys,
    cache_values,
    cache_length,
    ancestors,
    accepted_path,
    gate_up_weight,
    down_weight,
    draft_weight,
    draft_bias,
    vocab_weight,
    candidate_tokens,
):
    tok_block = hidden_state.shape[0]
    kv_count = lax.axis_size("kv")
    tenants = lax.axis_size("vocab")
    tree_size = tok_block * kv_count
    own_state = hidden_state[:, 0, :]
    tenant_state = lax.all_gather(own_state, "kv", axis=0, tiled=True)
    tenant_float = tenant_state.astype(jnp.float32)
    scaled_input = (tenant_float * norm_pre_attention).astype(jnp.bfloat16)
    projected_rows = jnp.einsum(
        "td,dhc->thc", scaled_input, input_projection, preferred_element_type=jnp.float32
    )
    projected_rows, squares = lax.psum(
        (projected_rows, jnp.sum(tenant_float * tenant_float, axis=-1)), "seq"
    )
    projected_rows = projected_rows * lax.rsqrt(squares / MODEL_WIDTH + EPSILON)[:, None, None]
    head_count = projected_rows.shape[1]
    depths = jnp.sum(ancestors[0], axis=-1) - 1
    length = cache_length[0]
    token_positions = length + depths
    query_rows = apply_rotary(
        projected_rows[:, :, : 2 * HEAD_SIZE].reshape(tree_size, head_count, 2, HEAD_SIZE),
        token_positions[:, None, None],
    ).astype(jnp.bfloat16)
    new_keys = apply_rotary(
        projected_rows[:, :, 2 * HEAD_SIZE : 3 * HEAD_SIZE], token_positions[:, None]
    ).astype(jnp.bfloat16)
    new_values = projected_rows[:, :, 3 * HEAD_SIZE :].astype(jnp.bfloat16)
    block_size = cache_keys.shape[1]
    block_start = lax.axis_index("seq") * block_size
    cache_cells = block_start + jnp.arange(block_size, dtype=jnp.int32)
    scores = jnp.einsum(
        "thgc,shc->thgs", query_rows, cache_keys[0], preferred_element_type=jnp.float32
    )
    weights = jnp.where((cache_cells < length)[None, None, None, :], capped_weight(scores), 0.0)
    numerator = jnp.einsum(
        "thgs,shc->thgc",
        weights.astype(jnp.bfloat16),
        cache_values[0],
        preferred_element_type=jnp.float32,
    )
    numerator, denominator = lax.psum((numerator, jnp.sum(weights, axis=-1)), "seq")
    tree_scores = jnp.einsum(
        "thgc,uhc->thgu", query_rows, new_keys, preferred_element_type=jnp.float32
    )
    tree_weights = jnp.where(ancestors[0][:, None, None, :] > 0, capped_weight(tree_scores), 0.0)
    numerator = numerator + jnp.einsum(
        "thgu,uhc->thgc",
        tree_weights.astype(jnp.bfloat16),
        new_values,
        preferred_element_type=jnp.float32,
    )
    denominator = denominator + jnp.sum(tree_weights, axis=-1)
    attended = (
        (numerator / denominator[..., None])
        .astype(jnp.bfloat16)
        .reshape(tree_size, head_count * 2 * HEAD_SIZE)
    )
    out_matrix = output_projection.reshape(head_count * 2 * HEAD_SIZE, output_projection.shape[2])
    attention_out = lax.psum_scatter(
        jnp.dot(attended, out_matrix, preferred_element_type=jnp.float32),
        "kv",
        scatter_dimension=0,
        tiled=True,
    )
    first_sum = (
        own_state.astype(jnp.float32)
        + attention_out * row_inverse(attention_out) * norm_post_attention
    ).astype(jnp.bfloat16)
    all_state = lax.all_gather(first_sum, ("kv", "vocab"), axis=0, tiled=True)
    all_float = all_state.astype(jnp.float32)
    scaled_ffn = (all_float * norm_pre_feedforward).astype(jnp.bfloat16)
    gate_up = jnp.einsum(
        "td,dcf->tcf", scaled_ffn, gate_up_weight, preferred_element_type=jnp.float32
    )
    ffn_squares = jnp.sum(all_float * all_float, axis=-1)
    gate_up, ffn_squares = lax.psum((gate_up, ffn_squares), "seq")
    activated = gated_units(gate_up, ffn_squares)
    ffn_out = lax.psum_scatter(
        jnp.dot(activated, down_weight, preferred_element_type=jnp.float32),
        ("kv", "vocab"),
        scatter_dimension=0,
        tiled=True,
    )
    first_float = first_sum.astype(jnp.float32)
    second_sum = (first_float + ffn_out * row_inverse(ffn_out) * norm_post_feedforward).astype(
        jnp.bfloat16
    )
    second_float = second_sum.astype(jnp.float32)
    normed = (second_float * row_inverse(second_float) * norm_final).astype(jnp.bfloat16)
    gathered = lax.all_gather(normed, ("kv", "vocab"), axis=0, tiled=True)
    lifted = jnp.einsum("td,ndc->tnc", gathered, draft_weight, preferred_element_type=jnp.float32)
    lifted = lax.psum(lifted.astype(jnp.bfloat16), "seq").astype(jnp.float32)
    branch = jax.nn.silu(lifted + draft_bias).astype(jnp.bfloat16)
    row_count = gathered.shape[0]
    vocab_rows = vocab_weight.shape[0]
    draft_count = branch.shape[1]
    columns = vocab_weight
    base_logits = lax.dot_general(
        lax.all_gather(gathered, "seq", axis=1, tiled=True),
        columns,
        (((1,), (1,)), ((), ())),
        preferred_element_type=jnp.float32,
    )
    columns = vocab_weight
    draft_extra = jnp.einsum(
        "tnc,vc->tnv",
        lax.all_gather(branch, ("kv", "vocab"), axis=2, tiled=True),
        columns,
        preferred_element_type=jnp.float32,
    )
    raw_logits = jnp.concatenate(
        [base_logits[:, None, :], base_logits[:, None, :] + draft_extra], axis=1
    )
    logits = LOGIT_CAP * jnp.tanh(raw_logits / LOGIT_CAP)
    totals = jnp.sum(jnp.exp(logits), axis=-1)
    head_total = draft_count + 1
    candidates = candidate_tokens.reshape(head_total, kv_count, tok_block, tenants, CAND)
    candidates = jnp.transpose(candidates, (0, 1, 3, 2, 4)).reshape(head_total, row_count, CAND)
    candidates = jnp.transpose(candidates, (1, 0, 2))
    vocab_start = lax.axis_index(("kv", "seq", "vocab")) * vocab_rows
    local_tokens = candidates - vocab_start
    entry_index = jnp.arange(vocab_rows, dtype=jnp.int32)
    picked = jnp.stack(
        [
            jnp.sum(
                jnp.where(entry_index == local_tokens[:, :, column : column + 1], logits, 0.0),
                axis=-1,
            )
            for column in range(CAND)
        ],
        axis=-1,
    )
    totals, picked = lax.psum((totals, picked), ("kv", "seq", "vocab"))
    log_totals = jnp.transpose(jnp.log(totals)).reshape(head_total, kv_count, tenants, tok_block)
    log_normalizer = jnp.transpose(log_totals, (0, 1, 3, 2)).reshape(head_total, tree_size, tenants)
    picked = jnp.transpose(picked, (1, 0, 2)).reshape(
        head_total, kv_count, tenants, tok_block, CAND
    )
    candidate_logits = jnp.transpose(picked, (0, 1, 3, 2, 4)).reshape(
        head_total, tree_size, tenants, CAND
    )
    accept_count = accepted_path.shape[1]
    slot_rows = length + jnp.arange(accept_count, dtype=jnp.int32)
    tree_nodes = jnp.arange(tree_size, dtype=jnp.int32)
    matches = (cache_cells[:, None, None] == slot_rows[None, :, None]) & (
        accepted_path[0][None, :, None] == tree_nodes[None, None, :]
    )
    selector = jnp.sum(matches.astype(jnp.float32), axis=1)
    written = jnp.sum(selector, axis=-1) > 0.0
    selector = selector.astype(jnp.bfloat16)

    def write_path(old_block, fresh_rows):
        moved_rows = jnp.dot(
            selector, fresh_rows.reshape(tree_size, -1), preferred_element_type=jnp.float32
        ).astype(jnp.bfloat16)
        return jnp.where(
            written[:, None], moved_rows, old_block[0].reshape(block_size, -1)
        ).reshape(old_block.shape)

    keys_updated = write_path(cache_keys, new_keys)
    values_updated = write_path(cache_values, new_values)
    return (keys_updated, values_updated, log_normalizer, candidate_logits)


def solution(mesh):
    placed = (
        P("kv", "vocab", "seq"),
        P("seq", "kv", None),
        P("kv", None, "seq"),
        P("seq"),
        P("seq"),
        P("seq"),
        P("seq"),
        P("seq"),
        P("vocab", "seq", "kv", None),
        P("vocab", "seq", "kv", None),
        P("vocab"),
        P("vocab", None, None),
        P("vocab", None),
        P("seq", None, ("kv", "vocab")),
        P(("kv", "vocab"), "seq"),
        P(None, "seq", ("kv", "vocab")),
        P(None, ("kv", "vocab")),
        P(("kv", "seq", "vocab"), None),
        P(),
    )
    return jax.shard_map(
        local,
        mesh=mesh,
        in_specs=placed,
        out_specs=(P("vocab", "seq", "kv", None), P("vocab", "seq", "kv", None), P(), P()),
        check_vma=False,
    )
```

profile of v0, /device:TPU:1, one launch (start us, length us, event | category | flops | bytes accessed | tf_op | source)
XLA Modules:
  0.0 775.7 jit_solution(17245792410160348582)
XLA Ops:
  7.2 0.8 copy.52
  8.1 15.8 %all-gather = bf16[48,1,448]{2,1,0:T(2,128)(2,1)S(1)} all-gather(bf16[6,1,448]{2,1,0:T(2,128)(2,1)S(1)} %copy.52), channel_id=2, replica_groups=mesh['kv'=8,'seq'=8,'vocab'=4] {'kv'}, dimensions={0}, use_global_device_ids=true | all-gather | bytes 48384 | tf_op jit(solution)/shard_map/all_gather | solution.py:73
  24.0 2.2 convolution_bitcast_fusion
  26.3 15.0 %psum.85 = f32[48]{0:T(128)S(1)} all-reduce(f32[48]{0:T(128)S(1)} %fusion.56), channel_id=1, replica_groups=mesh['kv'=8,'seq'=8,'vocab'=4] {'seq'}, use_global_device_ids=true, to_apply=%region_4.5 | all-reduce | flops 48 | bytes 384 | tf_op jit(solution)/shard_map/psum | solution.py:79
  42.7 0.8 reduce_sum.178
  43.9 50.6 %all-reduce.10.cloned.1.call-done = f32[48,1,1024]{2,0,1:T(8,128)} async-done(((f32[48,1,1024]{2,0,1:T(8,128)}), f32[48,1,1024]{2,0,1:T(8,128)}) %all-reduce.10.cloned.1.call-update) | async-done | bytes 196624 | tf_op jit(solution)/shard_map/psum | solution.py:79
  94.5 1.0 broadcast_multiply_fusion
  95.8 1.2 fusion.93
  97.1 12.7 %psum.87 = f32[48,1,2]{0,2,1:T(2,128)S(1)} all-reduce(f32[48,1,2]{0,2,1:T(2,128)S(1)} %bitcast.224), channel_id=1, replica_groups=mesh['kv'=8,'seq'=8,'vocab'=4] {'seq'}, use_global_device_ids=true, to_apply=%region_8.9 | all-reduce | flops 96 | bytes 768 | tf_op jit(solution)/shard_map/psum | solution.py:108
  109.8 2.0 convolution_bitcast_fusion.1
  112.0 73.8 %all-reduce.12.cloned.1.call-done = f32[48,1,2,256]{3,0,2,1:T(8,128)} async-done(((f32[48,1,2,256]{3,0,2,1:T(8,128)}), f32[48,1,2,256]{3,0,2,1:T(8,128)}) %all-reduce.12.cloned.1.call-update) | async-done | bytes 98320 | tf_op jit(solution)/shard_map/psum | solution.py:108
  185.8 1.1 fusion.24
  187.3 18.1 %fusion = f32[8,448]{1,0:T(8,128)S(1)} fusion(f32[48,448]{1,0:T(8,128)S(1)} %fusion.35), kind=kCustom, calls=%all-reduce-scatter | all-reduce-scatter fusion | flops 28673 | bytes 101376
  205.3 3.4 collective-permute-start
  208.8 1.6 collective-permute-start.1
  212.0 11.6 %psum.88 = f32[6]{0:T(128)S(1)} all-reduce(f32[6]{0:T(128)S(1)} %multiply_reduce_fusion.2), channel_id=1, replica_groups=mesh['kv'=8,'seq'=8,'vocab'=4] {'seq'}, use_global_device_ids=true, to_apply=%region_12.13 | all-reduce | flops 6 | bytes 48 | tf_op jit(solution)/shard_map/psum | solution.py:36
  223.7 45.5 %all-gather.1 = bf16[32,6,448]{2,1,0:T(8,128)(2,1)S(1)} all-gather(bf16[1,6,448]{2,1,0:T(8,128)(2,1)S(1)} %bitcast.223), channel_id=1, replica_groups=mesh['kv'=8,'seq'=8,'vocab'=4] {'kv','vocab'}, dimensions={0}, use_global_device_ids=true | all-gather | bytes 177408 | tf_op jit(solution)/shard_map/all_gather | solution.py:136
  269.4 1.3 fusion.33
  270.8 11.5 %psum.90 = f32[192]{0:T(256)S(1)} all-reduce(f32[192]{0:T(256)S(1)} %multiply_reduce_fusion), channel_id=1, replica_groups=mesh['kv'=8,'seq'=8,'vocab'=4] {'seq'}, use_global_device_ids=true, to_apply=%region_15.16 | all-reduce | flops 192 | bytes 1536 | tf_op jit(solution)/shard_map/psum | solution.py:143
  282.3 57.1 %all-reduce.14.cloned.1.call-done = f32[192,2,448]{2,0,1:T(8,128)} async-done(((f32[192,2,448]{2,0,1:T(8,128)}), f32[192,2,448]{2,0,1:T(8,128)}) %all-reduce.14.cloned.1.call-update) | async-done | bytes 688144 | tf_op jit(solution)/shard_map/psum | solution.py:143
  339.4 1.6 fusion.53
  341.1 68.1 %fusion.1 = f32[8,448]{1,0:T(8,128)S(1)} fusion(f32[192,448]{1,0:T(8,128)S(1)} %fusion.53), kind=kCustom, calls=%all-reduce-scatter.1 | all-reduce-scatter fusion | flops 114689 | bytes 359424
  409.1 1.9 collective-permute-start.2
  411.1 1.9 collective-permute-start.3
  413.0 1.4 collective-permute-start.9
  414.4 1.9 collective-permute-start.4
  416.4 1.9 collective-permute-start.5
  418.3 5.9 collective-permute-start.6
  424.2 6.8 collective-permute-start.7
  431.0 3.9 collective-permute-start.8
  437.2 12.6 %psum.91 = f32[6]{0:T(128)S(1)} all-reduce(f32[6]{0:T(128)S(1)} %multiply_reduce_fusion.1), channel_id=1, replica_groups=mesh['kv'=8,'seq'=8,'vocab'=4] {'seq'}, use_global_device_ids=true, to_apply=%region_18.19 | all-reduce | flops 6 | bytes 48 | tf_op jit(solution)/shard_map/psum | solution.py:36
  450.0 10.7 %psum.92 = f32[6]{0:T(128)S(1)} all-reduce(f32[6]{0:T(128)S(1)} %get-tuple-element.17), channel_id=1, replica_groups=mesh['kv'=8,'seq'=8,'vocab'=4] {'seq'}, use_global_device_ids=true, to_apply=%region_20.21 | all-reduce | flops 6 | bytes 48 | tf_op jit(solution)/shard_map/psum | solution.py:36
  460.8 48.2 %all-gather.2 = bf16[32,6,448]{2,1,0:T(8,128)(2,1)S(1)} all-gather(bf16[1,6,448]{2,1,0:T(8,128)(2,1)S(1)} %fusion.82), channel_id=1, replica_groups=mesh['kv'=8,'seq'=8,'vocab'=4] {'kv','vocab'}, dimensions={0}, use_global_device_ids=true | all-gather | bytes 177408 | tf_op jit(solution)/shard_map/all_gather | solution.py:157
  509.1 0.9 convolution_convert_fusion.2
  511.2 64.1 %all-reduce.16.cloned.1.call-done = bf16[192,4,112]{2,0,1:T(8,128)(2,1)} async-done(((bf16[192,4,112]{2,0,1:T(8,128)(2,1)}), bf16[192,4,112]{2,0,1:T(8,128)(2,1)}) %all-reduce.16.cloned.1.call-update) | async-done | bytes 172048 | tf_op jit(solution)/shard_map/psum | solution.py:159
  575.3 1.0 multiply_convert_fusion
  576.3 0.9 copy.60
  581.5 2.5 fusion.6
  584.1 1.5 fusion.8
  585.5 30.5 %all-gather.9.cloned.1.call-done = bf16[8,448,192]{1,2,0:T(8,128)(2,1)} async-done(((bf16[1,448,192]{1,2,0:T(8,128)(2,1)}), bf16[8,448,192]{1,2,0:T(8,128)(2,1)}) %all-gather.9.cloned.1.call-update) | async-done | bytes 1376272 | tf_op jit(solution)/shard_map/all_gather | solution.py:166
  616.1 2.3 copy.59
  618.4 2.7 reshape.412
  621.1 3.8 fusion.95
  625.0 52.4 %all-gather.7.cloned.1.call-done = bf16[192,4,3584]{0,1,2:T(4,128)(2,1)} async-done(((bf16[192,4,112]{0,1,2:T(4,128)(2,1)}), bf16[192,4,3584]{0,1,2:T(4,128)(2,1)}) %all-gather.7.cloned.1.call-update) | async-done | bytes 5505040 | tf_op jit(solution)/shard_map/all_gather | solution.py:174
  677.3 8.2 %fusion.17 = f32[192,4,512]{2,0,1:T(8,128)S(1)} fusion(bf16[512,3584]{1,0:T(8,128)(2,1)} %param.36, bf16[192,4,3584]{0,1,2:T(4,128)(2,1)} %all-gather.7.cloned.1.call-done, f32[192,512]{1,0:T(8,128)S(1)} %fusion.95), kind=kOutput, calls=%fused_computation.38 | convolution fusion | flops 2818965504 | bytes 11141120 | tf_op jit(solution)/shard_map/tnc,vc->tnv/dot_general | solution.py:172
  685.6 4.4 select_reduce_fusion
  690.2 0.8 reshape.400
  691.4 76.6 %all-reduce.4 = (f32[192,5]{0,1:T(8,128)S(1)}, f32[5,48,4,8]{1,3,2,0:T(8,128)}) all-reduce(f32[192,5]{0,1:T(8,128)S(1)} %get-tuple-element.19, f32[5,48,4,8]{1,3,2,0:T(8,128)S(1)} %reshape.401), channel_id=1, replica_groups=mesh['kv'=8,'seq'=8,'vocab'=4] {'kv','seq','vocab'}, use_global_device_ids=true, to_apply=%region_23.24 | all-reduce | flops 8640 | bytes 69120 | tf_op jit(solution)/shard_map/psum | solution.py:200
  (134 shorter events, 12.1 us)
Async XLA Ops:
  7.2 262.2 %copy-start = (bf16[448,2,448]{2,1,0:T(2,128)(2,1)S(1)}, bf16[448,2,448]{2,1,0:T(2,128)(2,1)}, u32[]{:S(2)}) copy-start(bf16[448,2,448]{2,1,0:T(2,128)(2,1)} %param.32) | copy-start | bytes 2408452
  7.2 88.7 %copy-start.2 = (bf16[1,2048,1,256]{3,1,2,0:T(8,128)(2,1)S(1)}, bf16[1,2048,1,256]{3,1,2,0:T(8,128)(2,1)}, u32[]{:S(2)}) copy-start(bf16[1,2048,1,256]{3,1,2,0:T(8,128)(2,1)} %param.27) | copy-start | bytes 3145732
  7.2 87.3 %all-reduce.10.cloned.1.call-start = ((), (), s32[]{:S(2)}) async-start(), calls=%async_computation | async-start | bytes 393216 | tf_op jit(solution)/shard_map/psum | solution.py:79
  26.1 83.6 %copy-start.1 = (bf16[1,2048,1,256]{3,1,2,0:T(8,128)(2,1)S(1)}, bf16[1,2048,1,256]{3,1,2,0:T(8,128)(2,1)}, u32[]{:S(2)}) copy-start(bf16[1,2048,1,256]{3,1,2,0:T(8,128)(2,1)} %param.28) | copy-start | bytes 3145732
  26.2 159.7 %all-reduce.12.cloned.1.call-start = ((), (), s32[]{:S(2)}) async-start(), calls=%async_computation.1 | async-start | bytes 196608 | tf_op jit(solution)/shard_map/psum | solution.py:108
  97.1 89.9 %copy-start.3 = (bf16[1,512,448]{1,2,0:T(8,128)(2,1)S(1)}, bf16[1,512,448]{1,2,0:T(8,128)(2,1)}, u32[]{:S(2)}) copy-start(bf16[1,512,448]{1,2,0:T(8,128)(2,1)} %param.21) | copy-start | bytes 1376260
  97.1 113.3 %copy-start.20 = (u32[256]{0:T(256)S(1)}, u32[256]{0:T(256)}, u32[]{:S(2)}) copy-start(u32[256]{0:T(256)} %constant.87) | copy-start | bytes 3076
  97.1 126.5 %copy-start.13 = (bf16[6,1,448]{2,0,1:T(8,128)(2,1)S(1)}, bf16[6,1,448]{2,0,1:T(8,128)(2,1)}, u32[]{:S(2)}) copy-start(bf16[6,1,448]{2,0,1:T(8,128)(2,1)} %param.19) | copy-start | bytes 16132
  97.1 126.5 %copy-start.16 = (f32[448]{0:T(512)S(1)}, f32[448]{0:T(512)}, u32[]{:S(2)}) copy-start(f32[448]{0:T(512)} %param.23) | copy-start | bytes 5380
  109.8 159.6 %copy-start.14 = (f32[448]{0:T(512)S(1)}, f32[448]{0:T(512)}, u32[]{:S(2)}) copy-start(f32[448]{0:T(512)} %param.24) | copy-start | bytes 5380
  111.8 227.7 %all-reduce.14.cloned.1.call-start = ((), (), s32[]{:S(2)}) async-start(), calls=%async_computation.2 | async-start | bytes 1572864 | tf_op jit(solution)/shard_map/psum | solution.py:143
  205.3 6.3 collective-permute-start
  208.8 2.8 collective-permute-start.1
  270.6 164.4 %copy-start.19 = (u32[256]{0:T(256)S(1)}, u32[256]{0:T(256)}, u32[]{:S(2)}) copy-start(u32[256]{0:T(256)} %constant.91) | copy-start | bytes 3076
  270.6 179.2 %copy-start.17 = (f32[448]{0:T(512)S(1)}, f32[448]{0:T(512)}, u32[]{:S(2)}) copy-start(f32[448]{0:T(512)} %param.25) | copy-start | bytes 5380
  270.6 190.1 %copy-start.18 = (f32[448]{0:T(512)S(1)}, f32[448]{0:T(512)}, u32[]{:S(2)}) copy-start(f32[448]{0:T(512)} %param.26) | copy-start | bytes 5380
  270.6 238.5 %copy-start.4 = (bf16[4,448,112]{2,1,0:T(8,128)(2,1)S(1)}, bf16[4,448,112]{2,1,0:T(8,128)(2,1)}, u32[]{:S(2)}) copy-start(bf16[4,448,112]{2,1,0:T(8,128)(2,1)} %param.34) | copy-start | bytes 1204228
  270.7 304.6 %all-reduce.16.cloned.1.call-start = ((), (), s32[]{:S(2)}) async-start(), calls=%async_computation.3 | async-start | bytes 393216 | tf_op jit(solution)/shard_map/psum | solution.py:159
  341.1 234.2 %copy-start.15 = (f32[4,112]{1,0:T(4,128)S(1)}, f32[4,112]{1,0:T(4,128)}, u32[]{:S(2)}) copy-start(f32[4,112]{1,0:T(4,128)} %param.35) | copy-start | bytes 5380
  409.1 15.1 %collective-permute-start.2 = (f32[8,448]{1,0:T(8,128)S(1)}, f32[8,448]{1,0:T(8,128)S(1)}, u32[]{:S(2)}, u32[]{:S(2)}) collective-permute-start(f32[8,448]{1,0:T(8,128)S(1)} %fusion.1), channel_id=1, source_target_pairs={{0,1},{1,2},{2,3},{3,32},{32,33},{33,34},{34,35},{35,64},{64,65},{... | collective-permute-start | bytes 43016
  411.1 20.0 %collective-permute-start.3 = (f32[8,448]{1,0:T(8,128)S(1)}, f32[8,448]{1,0:T(8,128)S(1)}, u32[]{:S(2)}, u32[]{:S(2)}) collective-permute-start(f32[8,448]{1,0:T(8,128)S(1)} %fusion.1), channel_id=1, source_target_pairs={{0,2},{1,3},{2,32},{3,33},{32,34},{33,35},{34,64},{35,65},{64,66},... | collective-permute-start | bytes 43016
  413.0 164.3 %copy-start.5 = (s32[5,48,4,8]{1,3,2,0:T(8,128)S(1)}, s32[5,48,4,8]{1,3,2,0:T(8,128)}, u32[]{:S(2)}) copy-start(s32[5,48,4,8]{1,3,2,0:T(8,128)} %param.37) | copy-start | bytes 92164
  413.0 5.3 collective-permute-start.9
  414.4 21.8 %collective-permute-start.4 = (f32[8,448]{1,0:T(8,128)S(1)}, f32[8,448]{1,0:T(8,128)S(1)}, u32[]{:S(2)}, u32[]{:S(2)}) collective-permute-start(f32[8,448]{1,0:T(8,128)S(1)} %fusion.1), channel_id=1, source_target_pairs={{0,3},{1,32},{2,33},{3,34},{32,35},{33,64},{34,65},{35,66},{64,67}... | collective-permute-start | bytes 43016
  416.4 19.9 %collective-permute-start.5 = (f32[8,448]{1,0:T(8,128)S(1)}, f32[8,448]{1,0:T(8,128)S(1)}, u32[]{:S(2)}, u32[]{:S(2)}) collective-permute-start(f32[8,448]{1,0:T(8,128)S(1)} %fusion.1), channel_id=1, source_target_pairs={{0,32},{1,33},{2,34},{3,35},{32,64},{33,65},{34,66},{35,67},{64,96... | collective-permute-start | bytes 43016
  418.3 17.9 %collective-permute-start.6 = (f32[8,448]{1,0:T(8,128)S(1)}, f32[8,448]{1,0:T(8,128)S(1)}, u32[]{:S(2)}, u32[]{:S(2)}) collective-permute-start(f32[8,448]{1,0:T(8,128)S(1)} %fusion.1), channel_id=1, source_target_pairs={{0,33},{1,34},{2,35},{3,64},{32,65},{33,66},{34,67},{35,96},{64,97... | collective-permute-start | bytes 43016
  424.2 12.1 %collective-permute-start.7 = (f32[8,448]{1,0:T(8,128)S(1)}, f32[8,448]{1,0:T(8,128)S(1)}, u32[]{:S(2)}, u32[]{:S(2)}) collective-permute-start(f32[8,448]{1,0:T(8,128)S(1)} %fusion.1), channel_id=1, source_target_pairs={{0,34},{1,35},{2,64},{3,65},{32,66},{33,67},{34,96},{35,97},{64,98... | collective-permute-start | bytes 43016
  431.0 5.2 collective-permute-start.8
  510.1 106.0 %all-gather.9.cloned.1.call-start = ((), (), s32[]{:S(2)}) async-start(), calls=%async_computation.5 | async-start | bytes 1769472 | tf_op jit(solution)/shard_map/all_gather | solution.py:166
  511.0 67.6 %copy-start.21 = (s32[1,5]{1,0:T(1,128)S(1)}, s32[1,5]{1,0:T(1,128)}, u32[]{:S(2)}) copy-start(s32[1,5]{1,0:T(1,128)} %param.31) | copy-start | bytes 64
  511.0 166.3 %all-gather.7.cloned.1.call-start = ((), (), s32[]{:S(2)}) async-start(), calls=%async_computation.4 | async-start | bytes 7569408 | tf_op jit(solution)/shard_map/all_gather | solution.py:174
  624.9 60.7 %copy-start.6 = (s32[192,5]{0,1:T(8,128)S(1)}, s32[192,5]{0,1:T(8,128)}, u32[]{:S(2)}) copy-start(s32[192,5]{0,1:T(8,128)} %get-tuple-element.43) | copy-start | bytes 11524
  624.9 60.7 %copy-start.7 = (s32[192,5]{0,1:T(8,128)S(1)}, s32[192,5]{0,1:T(8,128)}, u32[]{:S(2)}) copy-start(s32[192,5]{0,1:T(8,128)} %get-tuple-element.44) | copy-start | bytes 11524
  624.9 60.7 %copy-start.8 = (s32[192,5]{0,1:T(8,128)S(1)}, s32[192,5]{0,1:T(8,128)}, u32[]{:S(2)}) copy-start(s32[192,5]{0,1:T(8,128)} %get-tuple-element.45) | copy-start | bytes 11524
  624.9 60.7 %copy-start.9 = (s32[192,5]{0,1:T(8,128)S(1)}, s32[192,5]{0,1:T(8,128)}, u32[]{:S(2)}) copy-start(s32[192,5]{0,1:T(8,128)} %get-tuple-element.46) | copy-start | bytes 11524
  624.9 60.7 %copy-start.10 = (s32[192,5]{0,1:T(8,128)S(1)}, s32[192,5]{0,1:T(8,128)}, u32[]{:S(2)}) copy-start(s32[192,5]{0,1:T(8,128)} %get-tuple-element.47) | copy-start | bytes 11524
  624.9 60.7 %copy-start.11 = (s32[192,5]{0,1:T(8,128)S(1)}, s32[192,5]{0,1:T(8,128)}, u32[]{:S(2)}) copy-start(s32[192,5]{0,1:T(8,128)} %get-tuple-element.48) | copy-start | bytes 11524
  625.0 60.7 %copy-start.12 = (s32[192,5]{0,1:T(8,128)S(1)}, s32[192,5]{0,1:T(8,128)}, u32[]{:S(2)}) copy-start(s32[192,5]{0,1:T(8,128)} %get-tuple-element.49) | copy-start | bytes 11524
Sparse Core Ops, SparseCore 0:
  26.3 68.1 all-reduce.9
  111.9 73.9 all-reduce.11
  270.8 68.6 all-reduce.13
  510.2 65.0 all-reduce.15
  576.9 39.1 all-gather.8
  618.5 58.7 all-gather.6
where the time goes:
time: 777 us; the launch traced here: 776 us
  blocking collectives  346 us (45%)
  waiting for transfers between devices  329 us (42%)
  starting transfers between devices  31.2 us (4%)
  matrix products  26.7 us (3%)
  between operations  16.9 us (2%)
  local copies, waits for them, and re-layouts  16 us (2%)
  other arithmetic  9.93 us (1%)
    unnamed x2, blocking collectives  86.2 us
    psum x1, blocking collectives, local(): totals, picked = lax.psum((totals, picked), ('kv', 'seq', 'vocab'))  76.6 us
    psum x1, waiting for transfers between devices, local(): lax.psum((numerator, jnp.sum(weights, axis=-1)), 'seq')  73.8 us
    psum x1, waiting for transfers between devices, local(): lifted = lax.psum(lifted.astype(jnp.bfloat16), 'seq').astype(jnp.float32)  64.1 us
    psum x1, waiting for transfers between devices, local(): gate_up, ffn_squares = lax.psum((gate_up, ffn_squares), 'seq')  57.1 us
    all_gather x1, waiting for transfers between devices, local(): lax.all_gather(branch, ('kv', 'vocab'), axis=2, tiled=True)  52.4 us
    psum x1, waiting for transfers between devices, local(): lax.psum((projected_rows, jnp.sum(tenant_float * tenant_float, axis=-1)),...  50.6 us
    all_gather x1, blocking collectives, local(): gathered = lax.all_gather(normed, ('kv', 'vocab'), axis=0, tiled=True)  48.2 us
  transfers between devices with their start and end apart: 16, of which 6 were waited for; matrix products, arithmetic and copies ran while one was open for 3% of the time, Pallas kernels for 0%

commit v1 on v0

--- a/solution.py
+++ b/solution.py
@@ -9,6 +9,27 @@
 EPSILON = 1e-06
 SCORE_CAP = 50.0
 LOGIT_CAP = 30.0
+
+
+def collect(array, axis, dim):
+    size, index, rows = (lax.axis_size(axis), lax.axis_index(axis), array.shape[dim])
+    right = [(i, (i + 1) % size) for i in range(size)]
+    behind = [(i, (i - 1) % size) for i in range(size)]
+    whole = jnp.zeros((*array.shape[:dim], size * rows, *array.shape[dim + 1 :]), array.dtype)
+    whole = lax.dynamic_update_slice_in_dim(whole, array, index * rows, axis=dim)
+    from_left = from_right = array
+    middle = size // 2
+    for hop in range(1, middle + 1):
+        from_left = lax.ppermute(from_left, axis, right)
+        whole = lax.dynamic_update_slice_in_dim(
+            whole, from_left, (index - hop) % size * rows, axis=dim
+        )
+        if hop < size - middle:
+            from_right = lax.ppermute(from_right, axis, behind)
+            whole = lax.dynamic_update_slice_in_dim(
+                whole, from_right, (index + hop) % size * rows, axis=dim
+            )
+    return whole
 
 
 def apply_rotary(vectors, token_positions):
@@ -163,7 +184,7 @@
     draft_count = branch.shape[1]
     columns = vocab_weight
     base_logits = lax.dot_general(
-        lax.all_gather(gathered, "seq", axis=1, tiled=True),
+        collect(gathered, "seq", 1),
         columns,
         (((1,), (1,)), ((), ())),
         preferred_element_type=jnp.float32,

time: 777 us -> 743 us (0.956)
  waiting for transfers between devices: 329 us -> 262 us
  local copies, waits for them, and re-layouts: 16 us -> 37.1 us
    all_gather x1, waiting for transfers between devices: 52.4 us -> 2.18 us  [local(): lax.all_gather(branch, ('kv', 'vocab'), axis=2, tiled=True)]
    all_gather x1 -> x0, waiting for transfers between devices: 30.5 us -> none  [local(): lax.all_gather(gathered, 'seq', axis=1, tiled=True)]
    dynamic_update_slice x0 -> x8, local copies, waits for them, and re-layouts: none -> 24.8 us  [the longest x4 12.1 us: collect(): lax.dynamic_update_slice_in_dim(whole, from_left, (index - hop) % size *...]
    ppermute x0 -> x7, waiting for transfers between devices: none -> 9.1 us  [the longest x4 8.41 us: collect(): from_left = lax.ppermute(from_left, axis, right)]
    ppermute x0 -> x7, starting transfers between devices: none -> 8.61 us  [the longest x3 7.77 us: collect(): from_right = lax.ppermute(from_right, axis, behind)]
  transfers between devices with their start and end apart: 16 -> 22, of which waited for: 6 -> 10; matrix products, arithmetic and copies ran while one was open for 3% -> 6% of each run, Pallas kernels for 0% -> 0%
where the time goes in v1:
time: 743 us; the launch traced here: 742 us
  blocking collectives  350 us (47%)
  waiting for transfers between devices  262 us (35%)
  starting transfers between devices  38.4 us (5%)
  local copies, waits for them, and re-layouts  37.1 us (5%)
  matrix products  26.9 us (4%)
  between operations  16.6 us (2%)
  other arithmetic  10.6 us (1%)
    unnamed x2, blocking collectives  86.2 us
    psum x1, blocking collectives, local(): totals, picked = lax.psum((totals, picked), ('kv', 'seq', 'vocab'))  82.8 us
    psum x1, waiting for transfers between devices, local(): lax.psum((numerator, jnp.sum(weights, axis=-1)), 'seq')  73.8 us
    psum x1, waiting for transfers between devices, local(): lifted = lax.psum(lifted.astype(jnp.bfloat16), 'seq').astype(jnp.float32)  66 us
    psum x1, waiting for transfers between devices, local(): gate_up, ffn_squares = lax.psum((gate_up, ffn_squares), 'seq')  57.1 us
    psum x1, waiting for transfers between devices, local(): lax.psum((projected_rows, jnp.sum(tenant_float * tenant_float, axis=-1)),...  50.6 us
    all_gather x1, blocking collectives, local(): gathered = lax.all_gather(normed, ('kv', 'vocab'), axis=0, tiled=True)  45.8 us
    all_gather x1, blocking collectives, local(): all_state = lax.all_gather(first_sum, ('kv', 'vocab'), axis=0, tiled=True)  45.5 us
  transfers between devices with their start and end apart: 22, of which 10 were waited for; matrix products, arithmetic and copies ran while one was open for 6% of the time, Pallas kernels for 0%

profile of v1, /device:TPU:1, one launch (start us, length us, event | category | flops | bytes accessed | tf_op | source)
XLA Modules:
  0.0 741.7 jit_solution(621480224853497654)
XLA Ops:
  8.1 15.8 %all-gather = bf16[48,1,448]{2,1,0:T(2,128)(2,1)S(1)} all-gather(bf16[6,1,448]{2,1,0:T(2,128)(2,1)S(1)} %copy.50), channel_id=2, replica_groups=mesh['kv'=8,'seq'=8,'vocab'=4] {'kv'}, dimensions={0}, use_global_device_ids=true | all-gather | bytes 48384 | tf_op jit(solution)/shard_map/all_gather | solution.py:94
  24.0 2.2 convolution_bitcast_fusion
  26.3 15.0 %psum.85 = f32[48]{0:T(128)S(1)} all-reduce(f32[48]{0:T(128)S(1)} %fusion.51), channel_id=1, replica_groups=mesh['kv'=8,'seq'=8,'vocab'=4] {'seq'}, use_global_device_ids=true, to_apply=%region_4.5 | all-reduce | flops 48 | bytes 384 | tf_op jit(solution)/shard_map/psum | solution.py:100
  43.9 50.6 %all-reduce.10.cloned.1.call-done = f32[48,1,1024]{2,0,1:T(8,128)} async-done(((f32[48,1,1024]{2,0,1:T(8,128)}), f32[48,1,1024]{2,0,1:T(8,128)}) %all-reduce.10.cloned.1.call-update) | async-done | bytes 196624 | tf_op jit(solution)/shard_map/psum | solution.py:100
  97.1 12.7 %psum.87 = f32[48,1,2]{0,2,1:T(2,128)S(1)} all-reduce(f32[48,1,2]{0,2,1:T(2,128)S(1)} %bitcast.218), channel_id=1, replica_groups=mesh['kv'=8,'seq'=8,'vocab'=4] {'seq'}, use_global_device_ids=true, to_apply=%region_8.9 | all-reduce | flops 96 | bytes 768 | tf_op jit(solution)/shard_map/psum | solution.py:129
  109.8 2.0 convolution_bitcast_fusion.1
  112.1 73.8 %all-reduce.12.cloned.1.call-done = f32[48,1,2,256]{3,0,2,1:T(8,128)} async-done(((f32[48,1,2,256]{3,0,2,1:T(8,128)}), f32[48,1,2,256]{3,0,2,1:T(8,128)}) %all-reduce.12.cloned.1.call-update) | async-done | bytes 98320 | tf_op jit(solution)/shard_map/psum | solution.py:129
  187.3 18.1 %fusion = f32[8,448]{1,0:T(8,128)S(1)} fusion(f32[48,448]{1,0:T(8,128)S(1)} %fusion.30), kind=kCustom, calls=%all-reduce-scatter | all-reduce-scatter fusion | flops 28673 | bytes 101376
  205.4 3.4 collective-permute-start.7
  212.0 11.6 %psum.88 = f32[6]{0:T(128)S(1)} all-reduce(f32[6]{0:T(128)S(1)} %multiply_reduce_fusion.2), channel_id=1, replica_groups=mesh['kv'=8,'seq'=8,'vocab'=4] {'seq'}, use_global_device_ids=true, to_apply=%region_12.13 | all-reduce | flops 6 | bytes 48 | tf_op jit(solution)/shard_map/psum | solution.py:57
  223.7 45.5 %all-gather.1 = bf16[32,6,448]{2,1,0:T(8,128)(2,1)S(1)} all-gather(bf16[1,6,448]{2,1,0:T(8,128)(2,1)S(1)} %bitcast.217), channel_id=1, replica_groups=mesh['kv'=8,'seq'=8,'vocab'=4] {'kv','vocab'}, dimensions={0}, use_global_device_ids=true | all-gather | bytes 177408 | tf_op jit(solution)/shard_map/all_gather | solution.py:157
  270.8 11.5 %psum.90 = f32[192]{0:T(256)S(1)} all-reduce(f32[192]{0:T(256)S(1)} %multiply_reduce_fusion), channel_id=1, replica_groups=mesh['kv'=8,'seq'=8,'vocab'=4] {'seq'}, use_global_device_ids=true, to_apply=%region_15.16 | all-reduce | flops 192 | bytes 1536 | tf_op jit(solution)/shard_map/psum | solution.py:164
  282.4 57.1 %all-reduce.14.cloned.1.call-done = f32[192,2,448]{2,0,1:T(8,128)} async-done(((f32[192,2,448]{2,0,1:T(8,128)}), f32[192,2,448]{2,0,1:T(8,128)}) %all-reduce.14.cloned.1.call-update) | async-done | bytes 688144 | tf_op jit(solution)/shard_map/psum | solution.py:164
  339.5 1.6 fusion.48
  341.1 68.1 %fusion.1 = f32[8,448]{1,0:T(8,128)S(1)} fusion(f32[192,448]{1,0:T(8,128)S(1)} %fusion.48), kind=kCustom, calls=%all-reduce-scatter.1 | all-reduce-scatter fusion | flops 114689 | bytes 359424
  409.2 1.9 collective-permute-start.10
  411.1 1.9 collective-permute-start.11
  414.3 1.9 collective-permute-start.12
  416.3 3.1 collective-permute-start.13
  419.4 7.2 collective-permute-start.14
  426.6 5.3 collective-permute-start.15
  431.9 1.9 collective-permute-start.9
  435.1 3.0 collective-permute-done.9
  439.1 12.6 %psum.91 = f32[6]{0:T(128)S(1)} all-reduce(f32[6]{0:T(128)S(1)} %multiply_reduce_fusion.1), channel_id=1, replica_groups=mesh['kv'=8,'seq'=8,'vocab'=4] {'seq'}, use_global_device_ids=true, to_apply=%region_18.19 | all-reduce | flops 6 | bytes 48 | tf_op jit(solution)/shard_map/psum | solution.py:57
  451.9 10.7 %psum.92 = f32[6]{0:T(128)S(1)} all-reduce(f32[6]{0:T(128)S(1)} %get-tuple-element.17), channel_id=1, replica_groups=mesh['kv'=8,'seq'=8,'vocab'=4] {'seq'}, use_global_device_ids=true, to_apply=%region_20.21 | all-reduce | flops 6 | bytes 48 | tf_op jit(solution)/shard_map/psum | solution.py:57
  462.7 45.8 %all-gather.2 = bf16[32,6,448]{2,1,0:T(8,128)(2,1)S(1)} all-gather(bf16[1,6,448]{2,1,0:T(8,128)(2,1)S(1)} %fusion.77), channel_id=1, replica_groups=mesh['kv'=8,'seq'=8,'vocab'=4] {'kv','vocab'}, dimensions={0}, use_global_device_ids=true | all-gather | bytes 177408 | tf_op jit(solution)/shard_map/all_gather | solution.py:178
  509.7 66.0 %all-reduce.16.cloned.1.call-done = bf16[192,4,112]{2,0,1:T(8,128)(2,1)} async-done(((bf16[192,4,112]{2,0,1:T(8,128)(2,1)}), bf16[192,4,112]{2,0,1:T(8,128)(2,1)}) %all-reduce.16.cloned.1.call-update) | async-done | bytes 172048 | tf_op jit(solution)/shard_map/psum | solution.py:180
  585.4 2.0 collective-permute-start.1
  587.4 1.9 collective-permute-done
  590.0 3.1 collective-permute-start.3
  593.1 4.2 collective-permute-done.2
  597.2 2.3 fusion.8
  599.6 2.7 collective-permute-start.5
  602.2 2.3 collective-permute-done.4
  604.5 2.2 fusion.6
  606.9 2.4 dynamic_update_slice.24
  609.3 2.3 dynamic_update_slice.25
  611.7 3.6 dynamic_update_slice.26
  615.3 3.0 dynamic_update_slice.27
  618.3 3.1 dynamic_update_slice.28
  621.4 3.6 dynamic_update_slice.29
  625.0 3.6 dynamic_update_slice.30
  628.6 3.1 dynamic_update_slice.31
  631.8 3.4 fusion.90
  635.3 2.2 all-gather.5.cloned.1.call-done
  637.5 8.2 %broadcast_add_fusion = f32[192,4,512]{2,0,1:T(8,128)S(1)} fusion(f32[192,512]{1,0:T(8,128)S(1)} %fusion.90, bf16[512,3584]{1,0:T(8,128)(2,1)} %param.36, bf16[192,4,3584]{0,1,2:T(4,128)(2,1)} %all-gather.5.cloned.1.call-done), kind=kOutput, calls=%fused_computation.56 | convolution fusion | flops 2818965504 | bytes 11141120 | tf_op jit(solution)/shard_map/tnc,vc->tnv/dot_general | solution.py:193
  645.8 4.4 select_reduce_fusion
  651.5 82.8 %all-reduce.4 = (f32[192,5]{0,1:T(8,128)S(1)}, f32[5,48,4,8]{1,3,2,0:T(8,128)}) all-reduce(f32[192,5]{0,1:T(8,128)S(1)} %get-tuple-element.19, f32[5,48,4,8]{1,3,2,0:T(8,128)S(1)} %reshape.401), channel_id=1, replica_groups=mesh['kv'=8,'seq'=8,'vocab'=4] {'kv','seq','vocab'}, use_global_device_ids=true, to_apply=%region_23.24 | all-reduce | flops 8640 | bytes 69120 | tf_op jit(solution)/shard_map/psum | solution.py:221
  (164 shorter events, 28.1 us)
Async XLA Ops:
  7.2 262.2 %copy-start = (bf16[448,2,448]{2,1,0:T(2,128)(2,1)S(1)}, bf16[448,2,448]{2,1,0:T(2,128)(2,1)}, u32[]{:S(2)}) copy-start(bf16[448,2,448]{2,1,0:T(2,128)(2,1)} %param.32) | copy-start | bytes 2408452
  7.2 88.7 %copy-start.2 = (bf16[1,2048,1,256]{3,1,2,0:T(8,128)(2,1)S(1)}, bf16[1,2048,1,256]{3,1,2,0:T(8,128)(2,1)}, u32[]{:S(2)}) copy-start(bf16[1,2048,1,256]{3,1,2,0:T(8,128)(2,1)} %param.27) | copy-start | bytes 3145732
  7.2 87.3 %all-reduce.10.cloned.1.call-start = ((), (), s32[]{:S(2)}) async-start(), calls=%async_computation | async-start | bytes 393216 | tf_op jit(solution)/shard_map/psum | solution.py:100
  26.1 83.7 %copy-start.1 = (bf16[1,2048,1,256]{3,1,2,0:T(8,128)(2,1)S(1)}, bf16[1,2048,1,256]{3,1,2,0:T(8,128)(2,1)}, u32[]{:S(2)}) copy-start(bf16[1,2048,1,256]{3,1,2,0:T(8,128)(2,1)} %param.28) | copy-start | bytes 3145732
  26.2 159.7 %all-reduce.12.cloned.1.call-start = ((), (), s32[]{:S(2)}) async-start(), calls=%async_computation.1 | async-start | bytes 196608 | tf_op jit(solution)/shard_map/psum | solution.py:129
  95.5 245.6 %copy-start.4 = (f32[48,1,1024]{2,0,1:T(8,128)}, f32[48,1,1024]{2,0,1:T(8,128)S(1)}, u32[]{:S(2)}) copy-start(f32[48,1,1024]{2,0,1:T(8,128)S(1)} %broadcast_multiply_fusion) | copy-start | bytes 589828
  95.7 16.1 %copy-start.10 = (bf16[48,128]{1,0:T(8,128)(2,1)}, bf16[48,128]{1,0:T(8,128)(2,1)S(1)}, u32[]{:S(2)}) copy-start(bf16[48,128]{1,0:T(8,128)(2,1)S(1)} %get-tuple-element.22) | copy-start | bytes 36868
  95.7 16.1 %copy-start.11 = (bf16[48,128]{1,0:T(8,128)(2,1)}, bf16[48,128]{1,0:T(8,128)(2,1)S(1)}, u32[]{:S(2)}) copy-start(bf16[48,128]{1,0:T(8,128)(2,1)S(1)} %get-tuple-element.23) | copy-start | bytes 36868
  97.1 89.9 %copy-start.5 = (bf16[1,512,448]{1,2,0:T(8,128)(2,1)S(1)}, bf16[1,512,448]{1,2,0:T(8,128)(2,1)}, u32[]{:S(2)}) copy-start(bf16[1,512,448]{1,2,0:T(8,128)(2,1)} %param.21) | copy-start | bytes 1376260
  97.1 113.3 %copy-start.27 = (u32[256]{0:T(256)S(1)}, u32[256]{0:T(256)}, u32[]{:S(2)}) copy-start(u32[256]{0:T(256)} %constant.142) | copy-start | bytes 3076
  97.1 126.5 %copy-start.20 = (bf16[6,1,448]{2,0,1:T(8,128)(2,1)S(1)}, bf16[6,1,448]{2,0,1:T(8,128)(2,1)}, u32[]{:S(2)}) copy-start(bf16[6,1,448]{2,0,1:T(8,128)(2,1)} %param.19) | copy-start | bytes 16132
  97.1 126.5 %copy-start.23 = (f32[448]{0:T(512)S(1)}, f32[448]{0:T(512)}, u32[]{:S(2)}) copy-start(f32[448]{0:T(512)} %param.23) | copy-start | bytes 5380
  109.8 159.6 %copy-start.21 = (f32[448]{0:T(512)S(1)}, f32[448]{0:T(512)}, u32[]{:S(2)}) copy-start(f32[448]{0:T(512)} %param.24) | copy-start | bytes 5380
  111.8 227.7 %all-reduce.14.cloned.1.call-start = ((), (), s32[]{:S(2)}) async-start(), calls=%async_computation.2 | async-start | bytes 1572864 | tf_op jit(solution)/shard_map/psum | solution.py:164
  205.4 6.3 collective-permute-start.7
  208.8 2.8 collective-permute-start.8
  270.6 163.2 %copy-start.26 = (u32[256]{0:T(256)S(1)}, u32[256]{0:T(256)}, u32[]{:S(2)}) copy-start(u32[256]{0:T(256)} %constant.146) | copy-start | bytes 3076
  270.6 181.1 %copy-start.24 = (f32[448]{0:T(512)S(1)}, f32[448]{0:T(512)}, u32[]{:S(2)}) copy-start(f32[448]{0:T(512)} %param.25) | copy-start | bytes 5380
  270.6 192.0 %copy-start.25 = (f32[448]{0:T(512)S(1)}, f32[448]{0:T(512)}, u32[]{:S(2)}) copy-start(f32[448]{0:T(512)} %param.26) | copy-start | bytes 5380
  270.7 238.0 %copy-start.6 = (bf16[4,448,112]{2,1,0:T(8,128)(2,1)S(1)}, bf16[4,448,112]{2,1,0:T(8,128)(2,1)}, u32[]{:S(2)}) copy-start(bf16[4,448,112]{2,1,0:T(8,128)(2,1)} %param.34) | copy-start | bytes 1204228
  270.7 305.0 %all-reduce.16.cloned.1.call-start = ((), (), s32[]{:S(2)}) async-start(), calls=%async_computation.3 | async-start | bytes 393216 | tf_op jit(solution)/shard_map/psum | solution.py:180
  282.4 293.3 %copy-start.22 = (f32[4,112]{1,0:T(4,128)S(1)}, f32[4,112]{1,0:T(4,128)}, u32[]{:S(2)}) copy-start(f32[4,112]{1,0:T(4,128)} %param.35) | copy-start | bytes 5380
  341.1 236.5 %copy-start.9 = (s32[5,48,4,8]{1,3,2,0:T(8,128)S(1)}, s32[5,48,4,8]{1,3,2,0:T(8,128)}, u32[]{:S(2)}) copy-start(s32[5,48,4,8]{1,3,2,0:T(8,128)} %param.37) | copy-start | bytes 92164
  409.2 17.4 %collective-permute-start.10 = (f32[8,448]{1,0:T(8,128)S(1)}, f32[8,448]{1,0:T(8,128)S(1)}, u32[]{:S(2)}, u32[]{:S(2)}) collective-permute-start(f32[8,448]{1,0:T(8,128)S(1)} %fusion.1), channel_id=1, source_target_pairs={{0,2},{1,3},{2,32},{3,33},{32,34},{33,35},{34,64},{35,65},{64,66},... | collective-permute-start | bytes 43016
  411.1 20.8 %collective-permute-start.11 = (f32[8,448]{1,0:T(8,128)S(1)}, f32[8,448]{1,0:T(8,128)S(1)}, u32[]{:S(2)}, u32[]{:S(2)}) collective-permute-start(f32[8,448]{1,0:T(8,128)S(1)} %fusion.1), channel_id=1, source_target_pairs={{0,3},{1,32},{2,33},{3,34},{32,35},{33,64},{34,65},{35,66},{64,67}... | collective-permute-start | bytes 43016
  413.0 6.3 collective-permute-start.16
  414.3 20.8 %collective-permute-start.12 = (f32[8,448]{1,0:T(8,128)S(1)}, f32[8,448]{1,0:T(8,128)S(1)}, u32[]{:S(2)}, u32[]{:S(2)}) collective-permute-start(f32[8,448]{1,0:T(8,128)S(1)} %fusion.1), channel_id=1, source_target_pairs={{0,32},{1,33},{2,34},{3,35},{32,64},{33,65},{34,66},{35,67},{64,96... | collective-permute-start | bytes 43016
  416.3 18.8 %collective-permute-start.13 = (f32[8,448]{1,0:T(8,128)S(1)}, f32[8,448]{1,0:T(8,128)S(1)}, u32[]{:S(2)}, u32[]{:S(2)}) collective-permute-start(f32[8,448]{1,0:T(8,128)S(1)} %fusion.1), channel_id=1, source_target_pairs={{0,33},{1,34},{2,35},{3,64},{32,65},{33,66},{34,67},{35,96},{64,97... | collective-permute-start | bytes 43016
  419.4 15.8 %collective-permute-start.14 = (f32[8,448]{1,0:T(8,128)S(1)}, f32[8,448]{1,0:T(8,128)S(1)}, u32[]{:S(2)}, u32[]{:S(2)}) collective-permute-start(f32[8,448]{1,0:T(8,128)S(1)} %fusion.1), channel_id=1, source_target_pairs={{0,34},{1,35},{2,64},{3,65},{32,66},{33,67},{34,96},{35,97},{64,98... | collective-permute-start | bytes 43016
  426.6 8.5 %collective-permute-start.15 = (f32[8,448]{1,0:T(8,128)S(1)}, f32[8,448]{1,0:T(8,128)S(1)}, u32[]{:S(2)}, u32[]{:S(2)}) collective-permute-start(f32[8,448]{1,0:T(8,128)S(1)} %fusion.1), channel_id=1, source_target_pairs={{0,35},{1,64},{2,65},{3,66},{32,67},{33,96},{34,97},{35,98},{64,99... | collective-permute-start | bytes 43016
  431.9 6.3 collective-permute-start.9
  509.6 127.8 %all-gather.5.cloned.1.call-start = ((), (), s32[]{:S(2)}) async-start(), calls=%async_computation.4 | async-start | bytes 7569408 | tf_op jit(solution)/shard_map/all_gather | solution.py:195
  579.6 25.0 %copy-start.3 = (bf16[1,2048,1,256]{3,1,2,0:T(8,128)(2,1)S(1)}, bf16[1,2048,1,256]{3,1,2,0:T(8,128)(2,1)}, u32[]{:S(2)}) copy-start(bf16[1,2048,1,256]{3,1,2,0:T(8,128)(2,1)} %param.27) | copy-start | bytes 3145732
  583.5 5.8 collective-permute-start
  585.4 4.6 collective-permute-start.1
  589.3 8.0 %collective-permute-start.2 = (bf16[192,448]{1,0:T(8,128)(2,1)S(1)}, bf16[192,448]{1,0:T(8,128)(2,1)S(1)}, u32[]{:S(2)}, u32[]{:S(2)}) collective-permute-start(bf16[192,448]{1,0:T(8,128)(2,1)S(1)} %collective-permute-done), channel_id=1, source_target_pairs={{0,4},{4,8},{8,12},{12,16},{16,20},{20,24},{24,28},{28,0},{1,5},{5... | collective-permute-start | bytes 516104 | tf_op jit(solution)/shard_map/ppermute | solution.py:23
  590.0 16.8 %copy-start.7 = (bf16[192,448]{1,0:T(8,128)(2,1)}, bf16[192,448]{1,0:T(8,128)(2,1)S(1)}, u32[]{:S(2)}) copy-start(bf16[192,448]{1,0:T(8,128)(2,1)S(1)} %collective-permute-done.1) | copy-start | bytes 516100
  590.0 9.6 %collective-permute-start.3 = (bf16[192,448]{1,0:T(8,128)(2,1)S(1)}, bf16[192,448]{1,0:T(8,128)(2,1)}, u32[]{:S(2)}, u32[]{:S(2)}) collective-permute-start(bf16[192,448]{1,0:T(8,128)(2,1)S(1)} %collective-permute-done.1), channel_id=1, source_target_pairs={{0,28},{4,0},{8,4},{12,8},{16,12},{20,16},{24,20},{28,24},{1,29},{... | collective-permute-start | bytes 516104 | tf_op jit(solution)/shard_map/ppermute | solution.py:28
  597.2 7.3 collective-permute-start.4
  599.6 25.5 %collective-permute-start.5 = (bf16[192,448]{1,0:T(8,128)(2,1)}, bf16[192,448]{1,0:T(8,128)(2,1)}, u32[]{:S(2)}, u32[]{:S(2)}) collective-permute-start(bf16[192,448]{1,0:T(8,128)(2,1)} %collective-permute-done.3), channel_id=1, source_target_pairs={{0,28},{4,0},{8,4},{12,8},{16,12},{20,16},{24,20},{28,24},{1,29},{... | collective-permute-start | bytes 516104 | tf_op jit(solution)/shard_map/ppermute | solution.py:28
  604.5 24.1 %collective-permute-start.6 = (bf16[192,448]{1,0:T(8,128)(2,1)}, bf16[192,448]{1,0:T(8,128)(2,1)}, u32[]{:S(2)}, u32[]{:S(2)}) collective-permute-start(bf16[192,448]{1,0:T(8,128)(2,1)} %collective-permute-done.4), channel_id=1, source_target_pairs={{0,4},{4,8},{8,12},{12,16},{16,20},{20,24},{24,28},{28,0},{1,5},{5... | collective-permute-start | bytes 516104 | tf_op jit(solution)/shard_map/ppermute | solution.py:23
  635.2 10.5 %copy-start.12 = (s32[192,5]{0,1:T(8,128)S(1)}, s32[192,5]{0,1:T(8,128)}, u32[]{:S(2)}) copy-start(s32[192,5]{0,1:T(8,128)} %get-tuple-element.42) | copy-start | bytes 11524
  635.2 10.5 %copy-start.13 = (s32[192,5]{0,1:T(8,128)S(1)}, s32[192,5]{0,1:T(8,128)}, u32[]{:S(2)}) copy-start(s32[192,5]{0,1:T(8,128)} %get-tuple-element.43) | copy-start | bytes 11524
  635.2 10.5 %copy-start.14 = (s32[192,5]{0,1:T(8,128)S(1)}, s32[192,5]{0,1:T(8,128)}, u32[]{:S(2)}) copy-start(s32[192,5]{0,1:T(8,128)} %get-tuple-element.44) | copy-start | bytes 11524
  635.2 10.5 %copy-start.15 = (s32[192,5]{0,1:T(8,128)S(1)}, s32[192,5]{0,1:T(8,128)}, u32[]{:S(2)}) copy-start(s32[192,5]{0,1:T(8,128)} %get-tuple-element.45) | copy-start | bytes 11524
  635.3 10.5 %copy-start.16 = (s32[192,5]{0,1:T(8,128)S(1)}, s32[192,5]{0,1:T(8,128)}, u32[]{:S(2)}) copy-start(s32[192,5]{0,1:T(8,128)} %get-tuple-element.46) | copy-start | bytes 11524
  635.3 10.5 %copy-start.17 = (s32[192,5]{0,1:T(8,128)S(1)}, s32[192,5]{0,1:T(8,128)}, u32[]{:S(2)}) copy-start(s32[192,5]{0,1:T(8,128)} %get-tuple-element.47) | copy-start | bytes 11524
  635.3 10.5 %copy-start.18 = (s32[192,5]{0,1:T(8,128)S(1)}, s32[192,5]{0,1:T(8,128)}, u32[]{:S(2)}) copy-start(s32[192,5]{0,1:T(8,128)} %get-tuple-element.48) | copy-start | bytes 11524
  (2 other events, 20.0 us)
Sparse Core Ops, SparseCore 0:
  26.3 68.1 all-reduce.9
  111.9 73.9 all-reduce.11
  270.8 68.6 all-reduce.13
  509.7 65.8 all-reduce.15
  578.1 59.2 all-gather.4
